TPU v7x, 32 devices: a whole 2x2x4 slice. The times are simulated.
32 devices in a mesh: pair: 2 (over core), lat: 4 (over y, x), tok: 4 (over z).
Axes of the slice: x: 2, y: 2, z: 4, core: 2. Of those that a mesh axis runs over, the one named last changes fastest.
Arguments:
- residual: bfloat16 [2, 512, 4096], P('pair', 'tok', 'lat'), may hold values from -6 to 6
- matches: int32 [2, 512], P('pair', 'tok'), may hold values from 0 to 511, as said below
- kl_grad: bfloat16 [512, 4096], P('tok', 'lat'), may hold values from -6 to 6
- active_blocks: int32 [64, 2], replicated, may hold values from 0 to 31, all different within a row; in each aligned block of 16 rows (0 to 15, 16 to 31, ...) at most 2 rows name the same one
- encoder: bfloat16 [4096, 4096], P(None, ('pair', 'lat', 'tok')), may hold values from -0.09375 to 0.09375
- encoder_offset_bias: float32 [4096], P(('pair', 'lat', 'tok')), may hold values from -3 to 3
- decoder: bfloat16 [4096, 4096], P(('pair', 'lat', 'tok')), may hold values from -0.5 to 0.5
- dec_bias: float32 [4096], P('lat'), may hold values from -3 to 3
Outputs:
- reconstruction: bfloat16 [512, 4096], P('tok', 'lat')
- scores: float32 [4096], P(('pair', 'lat', 'tok'))
Inputs may be any that keep to these rules, and one draw needn't show every extreme that they name: For each model m and matched token k: k - 128 < matches[m, k] <= k (at least 0); where k is a positive multiple of 128, matches[m, k] = k - 127. `active_blocks`: each row lists 2 different latent blocks. Among the 16 rows of one tok index (aligned blocks of rows) no latent block is listed more than 2 times, and some latent block is listed exactly 2 times.
All inputs are finite; a program needn't handle non-finite values.
Results may differ from a plain program's by a relative error of at most 0.0085.
Values may be sent and summed in bfloat16 or wider, within the bound.
A program may use at most 64 MiB of HBM per device.

v0:
```python
import math

import jax
import jax.numpy as jnp
from jax import lax
from jax.sharding import PartitionSpec as P

TBLK = 8
MOST = 2


def passed_along(x, axis, by):
    devices = lax.axis_size(axis)
    pairs = [(i, i + by) for i in range(devices) if 0 <= i + by < devices]
    return lax.ppermute(x, axis, pairs)


def from_partner(x, axis, bit):
    return lax.ppermute(x, axis, [(i, i ^ 1 << bit) for i in range(lax.axis_size(axis))])


def slot_table(my_lists, targets, slot_ids):
    listed = jnp.any(my_lists[:, :, None] == targets[None, None, :], axis=1).astype(jnp.int32)
    ranking = jnp.cumsum(listed, axis=0) - listed
    return (listed.T[:, None, :] * (ranking.T[:, None, :] == slot_ids[None, :, None])).astype(
        jnp.bfloat16
    )


def shards(
    residual, matches, kl_grad, active_blocks, encoder, encoder_offset_bias, decoder, dec_bias
):
    tok_dev = residual.shape[1]
    tok_count = lax.axis_size("tok")
    lat_count = lax.axis_size("lat")
    tok_here = lax.axis_index("tok")
    own_rows = residual[0]
    earlier = passed_along(own_rows, "tok", 1)
    window = jnp.concatenate([earlier, own_rows], axis=0)
    first_row = (tok_here - 1) * tok_dev
    local_index = matches[0] - first_row
    matched = jnp.take(window, local_index, axis=0)
    partner = from_partner(matched, "pair", 0)
    is_chat = lax.axis_index("pair") == 1
    chat_rows = jnp.where(is_chat, matched, partner)
    base_rows = jnp.where(is_chat, partner, matched)
    delta_rows = (chat_rows.astype(jnp.float32) - base_rows.astype(jnp.float32)).astype(
        jnp.bfloat16
    )
    tb_dev = tok_dev // TBLK
    pair_base = lax.axis_index("pair") * lat_count
    row_base = (pair_base + lax.axis_index("lat")) * tok_count
    my_block = row_base + tok_here
    my_lists = lax.dynamic_slice_in_dim(active_blocks, tok_here * tb_dev, tb_dev, 0)
    slot_ids = jnp.arange(MOST, dtype=jnp.int32)
    targets = row_base + jnp.arange(tok_count, dtype=jnp.int32)
    chooser = slot_table(my_lists, targets, slot_ids)
    mine_listed = jnp.any(active_blocks == my_block, axis=1).astype(jnp.int32)
    counts = jnp.sum(mine_listed.reshape(tok_count, tb_dev), axis=1)
    padded_output = (slot_ids[None, :] < counts[:, None]).astype(jnp.float32)[:, :, None, None]

    def select_slots(blocks):
        return jnp.einsum(
            "ksb,btd->kstd", chooser, blocks, preferred_element_type=jnp.float32
        ).astype(jnp.bfloat16)

    full_delta, full_grad = (
        lax.all_gather(delta_rows, "lat", axis=1, tiled=True),
        lax.all_gather(kl_grad, "lat", axis=1, tiled=True),
    )
    full_width = full_delta.shape[1]
    sent_delta = select_slots(full_delta.reshape(tb_dev, TBLK, full_width))
    sent_grad = select_slots(full_grad.reshape(tb_dev, TBLK, full_width))
    got_delta, got_grad = (
        lax.all_to_all(sent_delta, "tok", split_axis=0, concat_axis=0, tiled=True),
        lax.all_to_all(sent_grad, "tok", split_axis=0, concat_axis=0, tiled=True),
    )
    preactivation = jnp.einsum(
        "kstd,dc->kstc", got_delta, encoder, preferred_element_type=jnp.float32
    )
    gradient_inner_product = jnp.einsum(
        "kstd,cd->kstc", got_grad, decoder, preferred_element_type=jnp.float32
    )
    activation_value = jnp.maximum(preactivation + encoder_offset_bias, 0.0) * padded_output
    every_token_rows = tok_dev * tok_count
    scores = jnp.sum(activation_value * gradient_inner_product, axis=(0, 1, 2)) / math.sqrt(
        every_token_rows / 8
    )
    activation_half_precision = activation_value.astype(jnp.bfloat16)
    pieces_out = jnp.einsum(
        "fazg,gh->fazh", activation_half_precision, decoder, preferred_element_type=jnp.float32
    ).astype(jnp.bfloat16)
    returned = lax.all_to_all(pieces_out, "tok", split_axis=0, concat_axis=0, tiled=True)
    source_sums = jnp.einsum(
        "ksb,kstd->btd", chooser, returned, preferred_element_type=jnp.float32
    ).reshape(tok_dev, -1)
    shared = lax.psum_scatter(
        source_sums.astype(jnp.bfloat16), "lat", scatter_dimension=1, tiled=True
    )
    summed = lax.psum(shared, "pair").astype(jnp.float32)
    return ((summed + dec_bias).astype(jnp.bfloat16), scores)


def solution(mesh):
    placed = (
        P("pair", "tok", "lat"),
        P("pair", "tok"),
        P("tok", "lat"),
        P(),
        P(None, ("pair", "lat", "tok")),
        P(("pair", "lat", "tok")),
        P(("pair", "lat", "tok"), None),
        P("lat"),
    )
    return jax.shard_map(
        shards,
        mesh=mesh,
        in_specs=placed,
        out_specs=(P("tok", "lat"), P(("pair", "lat", "tok"))),
        check_vma=False,
    )
```

profile of v0, /device:TPU:0, one launch (start us, length us, event | category | flops | bytes accessed | tf_op | source)
XLA Modules:
  0.0 148.8 jit_solution(7111867988648437557)
XLA Ops:
  7.2 5.1 %collective-permute-start = (bf16[128,1024]{1,0:T(8,128)(2,1)}, bf16[128,1024]{1,0:T(8,128)(2,1)S(1)}, u32[]{:S(2)}, u32[]{:S(2)}) collective-permute-start(bf16[128,1024]{1,0:T(8,128)(2,1)} %bitcast.56), channel_id=1, source_target_pairs={{0,1},{1,2},{2,3},{4,5},{5,6},{6,7},{8,9},{9,10},{10,11},{12,13},{... | collective-permute-start | bytes 786440 | tf_op jit(solution)/shard_map/ppermute | solution.py:15
  12.3 0.7 fusion.20
  13.0 0.7 compare_and_fusion
  13.7 4.5 %collective-permute-done = bf16[128,1024]{1,0:T(8,128)(2,1)S(1)} collective-permute-done((bf16[128,1024]{1,0:T(8,128)(2,1)}, bf16[128,1024]{1,0:T(8,128)(2,1)S(1)}, u32[]{:S(2)}, u32[]{:S(2)}) %collective-permute-start) | collective-permute-done | bytes 262176 | tf_op jit(solution)/shard_map/ppermute | solution.py:15
  18.2 1.0 pad_maximum_fusion
  19.2 0.9 gather_fusion
  20.2 1.5 %collective-permute-done.1 = bf16[128,1024]{1,0:T(8,128)(2,1)S(1)} collective-permute-done((bf16[128,1024]{1,0:T(8,128)(2,1)S(1)}, bf16[128,1024]{1,0:T(8,128)(2,1)S(1)}, u32[]{:S(2)}, u32[]{:S(2)}) %collective-permute-start.1) | collective-permute-done | bytes 262176 | tf_op jit(solution)/shard_map/ppermute | solution.py:19
  21.7 0.9 subtract_convert_fusion
  23.2 28.2 %all-gather.3.cloned.1.call-done = bf16[128,4096]{1,0:T(8,128)(2,1)} async-done(((bf16[128,1024]{1,0:T(8,128)(2,1)}), bf16[128,4096]{1,0:T(8,128)(2,1)}) %all-gather.3.cloned.1.call-update) | async-done | bytes 1048592 | tf_op jit(solution)/shard_map/all_gather | solution.py:68
  51.4 2.5 %convolution_convert_fusion.1 = bf16[4,2,8,4096]{3,0,2,1:T(4,128)(2,1)S(1)} fusion(bf16[16,8,4096]{2,1,0:T(8,128)(2,1)} %bitcast.54, s32[4,16]{1,0:T(4,128)S(1)} %copy.50, s32[4,16]{1,0:T(4,128)S(1)} %copy.49), kind=kOutput, calls=%fused_computation.4 | convolution fusion | flops 8651136 | bytes 1573376 | tf_op jit(solution)/shard_map/ksb,btd->kstd/dot_general | solution.py:63
  53.9 1.1 copy.52
  55.0 4.6 %all-to-all-start = ((bf16[4,2,8,4096]{3,2,1,0:T(8,128)(2,1)}), bf16[4,2,8,4096]{3,2,1,0:T(8,128)(2,1)S(1)}, u32[]{:S(2)}, u32[]{:S(2)}) async-start(bf16[4,2,8,4096]{3,2,1,0:T(8,128)(2,1)} %copy.52), calls=%async_computation | async-start | bytes 1048576 | tf_op jit(solution)/shard_map/all_to_all | solution.py:75
  59.6 0.7 all-gather.5.cloned.1.call-update
  60.7 13.2 %all-to-all-done = bf16[4,2,8,4096]{3,2,1,0:T(8,128)(2,1)S(1)} async-done(((bf16[4,2,8,4096]{3,2,1,0:T(8,128)(2,1)}), bf16[4,2,8,4096]{3,2,1,0:T(8,128)(2,1)S(1)}, u32[]{:S(2)}, u32[]{:S(2)}) %all-to-all-start) | async-done | bytes 524320 | tf_op jit(solution)/shard_map/all_to_all | solution.py:75
  74.5 0.5 copy.54
  75.1 16.4 %all_to_all.15 = bf16[4,2,8,4096]{3,1,2,0:T(2,128)(2,1)S(1)} all-to-all(bf16[4,2,8,4096]{3,1,2,0:T(2,128)(2,1)S(1)} %copy.54), channel_id=1, replica_groups=mesh['pair'=2,'lat'=4,'tok'=4] {'tok'}, dimensions={0} | all-to-all | bytes 1048576 | tf_op jit(solution)/shard_map/all_to_all | solution.py:93
  91.5 0.7 fusion
  92.2 1.6 %copy.76 = bf16[16,8,4096]{2,1,0:T(8,128)(2,1)} copy(bf16[16,8,4096]{2,0,1:T(8,128)(2,1)S(1)} %fusion) | data formatting | bytes 2097152 | tf_op jit(solution)/shard_map/convert_element_type | solution.py:98
  93.9 2.5 %convolution_convert_fusion = bf16[4,2,8,4096]{3,0,2,1:T(4,128)(2,1)S(1)} fusion(bf16[16,8,4096]{2,1,0:T(8,128)(2,1)} %bitcast.55, s32[4,16]{1,0:T(4,128)S(1)} %copy.50, s32[4,16]{1,0:T(4,128)S(1)} %copy.49), kind=kOutput, calls=%fused_computation.3 | convolution fusion | flops 8651136 | bytes 1573376 | tf_op jit(solution)/shard_map/ksb,btd->kstd/dot_general | solution.py:63
  96.3 1.1 copy.58
  97.4 3.5 %all-to-all-start.2 = ((bf16[4,2,8,4096]{3,2,1,0:T(8,128)(2,1)}), bf16[4,2,8,4096]{3,2,1,0:T(8,128)(2,1)S(1)}, u32[]{:S(2)}, u32[]{:S(2)}) async-start(bf16[4,2,8,4096]{3,2,1,0:T(8,128)(2,1)} %copy.58), calls=%async_computation.3 | async-start | bytes 1048576 | tf_op jit(solution)/shard_map/all_to_all | solution.py:76
  101.0 19.1 %reduce-scatter.2.cloned.1.call-done = bf16[128,1024]{1,0:T(8,128)(2,1)} async-done(((bf16[128,4096]{1,0:T(8,128)(2,1)}), bf16[128,1024]{1,0:T(8,128)(2,1)}) %reduce-scatter.2.cloned.1.call-update) | async-done | bytes 262160 | tf_op jit(solution)/shard_map/reduce_scatter | solution.py:97
  121.1 19.4 %all-reduce.2.cloned.1.call-done = bf16[128,1024]{1,0:T(8,128)(2,1)} async-done(((bf16[128,1024]{1,0:T(8,128)(2,1)}), bf16[128,1024]{1,0:T(8,128)(2,1)}) %all-reduce.2.cloned.1.call-update) | async-done | bytes 262160 | tf_op jit(solution)/shard_map/psum | solution.py:100
  140.5 1.7 %add_convert_fusion = bf16[128,1024]{1,0:T(8,128)(2,1)} fusion(bf16[128,1024]{1,0:T(8,128)(2,1)} %all-reduce.2.cloned.1.call-done, f32[1024]{0:T(1024)S(1)} %copy-done.2), kind=kLoop, calls=%fused_computation.21 | loop fusion | flops 393216 | bytes 528384 | tf_op jit(solution)/shard_map/convert_element_type | solution.py:101
  (40 shorter events, 2.8 us)
Async XLA Ops:
  7.2 67.0 %copy-start = (bf16[128,4096]{1,0:T(8,128)(2,1)S(1)}, bf16[128,4096]{1,0:T(8,128)(2,1)}, u32[]{:S(2)}) copy-start(bf16[128,4096]{1,0:T(8,128)(2,1)} %param.14) | copy-start | bytes 3145732
  7.2 44.2 %all-gather.3.cloned.1.call-start = ((), (), s32[]{:S(2)}) async-start(), calls=%async_computation.4 | async-start | bytes 1310720 | tf_op jit(solution)/shard_map/all_gather | solution.py:68
  7.2 11.0 %collective-permute-start = (bf16[128,1024]{1,0:T(8,128)(2,1)}, bf16[128,1024]{1,0:T(8,128)(2,1)S(1)}, u32[]{:S(2)}, u32[]{:S(2)}) collective-permute-start(bf16[128,1024]{1,0:T(8,128)(2,1)} %bitcast.56), channel_id=1, source_target_pairs={{0,1},{1,2},{2,3},{4,5},{5,6},{6,7},{8,9},{9,10},{10,11},{12,13},{... | collective-permute-start | bytes 786440 | tf_op jit(solution)/shard_map/ppermute | solution.py:15
  20.0 2.7 %copy-start.3 = (s32[64,2]{0,1:T(2,128)S(1)}, s32[64,2]{0,1:T(2,128)}, u32[]{:S(2)}) copy-start(s32[64,2]{0,1:T(2,128)} %param.11) | copy-start | bytes 1540
  20.1 1.6 %collective-permute-start.1 = (bf16[128,1024]{1,0:T(8,128)(2,1)S(1)}, bf16[128,1024]{1,0:T(8,128)(2,1)S(1)}, u32[]{:S(2)}, u32[]{:S(2)}) collective-permute-start(bf16[128,1024]{1,0:T(8,128)(2,1)S(1)} %broadcast_select_fusion), channel_id=1, source_target_pairs={{0,16},{16,0},{1,17},{17,1},{2,18},{18,2},{3,19},{19,3},{4,20},{20... | collective-permute-start | bytes 786440 | tf_op jit(solution)/shard_map/ppermute | solution.py:19
  53.8 20.1 %copy-start.1 = (bf16[4096,128]{1,0:T(8,128)(2,1)S(1)}, bf16[4096,128]{1,0:T(8,128)(2,1)}, u32[]{:S(2)}) copy-start(bf16[4096,128]{1,0:T(8,128)(2,1)} %param.12) | copy-start | bytes 3145732
  53.9 20.0 %copy-start.4 = (f32[128]{0:T(128)S(1)}, f32[128]{0:T(128)}, u32[]{:S(2)}) copy-start(f32[128]{0:T(128)} %param.13) | copy-start | bytes 1540
  55.0 18.9 %all-to-all-start = ((bf16[4,2,8,4096]{3,2,1,0:T(8,128)(2,1)}), bf16[4,2,8,4096]{3,2,1,0:T(8,128)(2,1)S(1)}, u32[]{:S(2)}, u32[]{:S(2)}) async-start(bf16[4,2,8,4096]{3,2,1,0:T(8,128)(2,1)} %copy.52), calls=%async_computation | async-start | bytes 1048576 | tf_op jit(solution)/shard_map/all_to_all | solution.py:75
  59.6 34.3 %all-gather.5.cloned.1.call-start = ((), (), s32[]{:S(2)}) async-start(), calls=%async_computation.7 | async-start | bytes 1310720 | tf_op jit(solution)/shard_map/all_gather | solution.py:69
  60.3 59.8 %reduce-scatter.2.cloned.1.call-start = ((), (), s32[]{:S(2)}) async-start(), calls=%async_computation.5 | async-start | bytes 1310720 | tf_op jit(solution)/shard_map/reduce_scatter | solution.py:97
  97.4 22.7 %all-to-all-start.2 = ((bf16[4,2,8,4096]{3,2,1,0:T(8,128)(2,1)}), bf16[4,2,8,4096]{3,2,1,0:T(8,128)(2,1)S(1)}, u32[]{:S(2)}, u32[]{:S(2)}) async-start(bf16[4,2,8,4096]{3,2,1,0:T(8,128)(2,1)} %copy.58), calls=%async_computation.3 | async-start | bytes 1048576 | tf_op jit(solution)/shard_map/all_to_all | solution.py:76
  100.9 39.6 %copy-start.2 = (f32[1024]{0:T(1024)S(1)}, f32[1024]{0:T(1024)}, u32[]{:S(2)}) copy-start(f32[1024]{0:T(1024)} %param.15) | copy-start | bytes 12292
  100.9 39.6 %all-reduce.2.cloned.1.call-start = ((), (), s32[]{:S(2)}) async-start(), calls=%async_computation.6 | async-start | bytes 524288 | tf_op jit(solution)/shard_map/psum | solution.py:100
Sparse Core Ops, SparseCore 0:
  22.8 28.5 all-gather.2
  62.2 26.9 all-gather.4
  94.0 26.0 reduce-scatter.1
  122.3 18.2 all-reduce.1
where the time goes:
time: 149 us
  waiting for transfers between devices  86.7 us (58%)
  blocking collectives  16.4 us (11%)
  between operations  13.9 us (9%)
  starting transfers between devices  13.4 us (9%)
  matrix products  6.75 us (5%)
  other arithmetic  5.9 us (4%)
  local copies, waits for them, and re-layouts  5.64 us (4%)
    all_gather x1, waiting for transfers between devices, shards(): lax.all_gather(delta_rows, 'lat', axis=1, tiled=True)  28.2 us
    psum x1, waiting for transfers between devices, shards(): summed = lax.psum(shared, 'pair').astype(jnp.float32)  19.4 us
    reduce_scatter x1, waiting for transfers between devices, shards(): lax.psum_scatter(source_sums.astype(jnp.bfloat16), 'lat', scatter_dimensi...  19.1 us
    all_to_all x1, blocking collectives, shards(): lax.all_to_all(pieces_out, 'tok', split_axis=0, concat_axis=0, tiled=True)  16.4 us
    all_to_all x1, waiting for transfers between devices, shards(): lax.all_to_all(sent_delta, 'tok', split_axis=0, concat_axis=0, tiled=True)  13.2 us
    ppermute x1, starting transfers between devices, passed_along(): return lax.ppermute(x, axis, pairs)  5.11 us
    dot_general x2, matrix products, select_slots(): jnp.einsum('ksb,btd->kstd', chooser, blocks, preferred_element_type=jnp.f...  4.93 us
    all_to_all x1, starting transfers between devices, shards(): lax.all_to_all(sent_delta, 'tok', split_axis=0, concat_axis=0, tiled=True)  4.6 us
  transfers between devices with their start and end apart: 8, of which 6 were waited for; matrix products, arithmetic and copies ran while one was open for 7% of the time, Pallas kernels for 0%

commit v1 on v0

--- a/solution.py
+++ b/solution.py
@@ -1,8 +1,11 @@
+import functools
 import math
 
 import jax
 import jax.numpy as jnp
 from jax import lax
+from jax.experimental import pallas as pl
+from jax.experimental.pallas import tpu as pltpu
 from jax.sharding import PartitionSpec as P
 
 TBLK = 8
@@ -101,6 +104,463 @@
     return ((summed + dec_bias).astype(jnp.bfloat16), scores)
 
 
+MESH = pl.DeviceIdType.MESH
+F32 = jnp.float32
+BF16 = jnp.bfloat16
+SLOT_ROWS = MOST * TBLK
+
+
+def remote(src, dst, send_sem, recv_sem, device):
+    return pltpu.make_async_remote_copy(
+        src_ref=src,
+        dst_ref=dst,
+        send_sem=send_sem,
+        recv_sem=recv_sem,
+        device_id=device,
+        device_id_type=MESH,
+    )
+
+
+def kernel(
+    PAIR,
+    LAT,
+    TOK,
+    residual,
+    matches,
+    grad,
+    act,
+    encoder,
+    enc_bias,
+    decoder,
+    dec_bias,
+    out,
+    scores,
+    win,
+    match_all,
+    part_out,
+    part_in,
+    own_delta,
+    delta_all,
+    grad_all,
+    choose,
+    sent_delta,
+    sent_grad,
+    got_delta,
+    got_grad,
+    fire,
+    pieces,
+    back,
+    sum_out,
+    sum_in,
+    enc_v,
+    dec_v,
+    local_sem,
+    win_sem,
+    match_send,
+    match_recv,
+    part_sem,
+    delta_send,
+    delta_recv,
+    grad_send,
+    grad_recv,
+    sd_send,
+    sd_recv,
+    sg_send,
+    sg_recv,
+    pc_send,
+    pc_recv,
+    sum_send,
+    sum_recv,
+    out_sem,
+):
+    p = lax.axis_index("pair")
+    l = lax.axis_index("lat")
+    t = lax.axis_index("tok")
+    rows, width = residual.shape
+    half = width // PAIR
+    group = PAIR * LAT
+    j = p * LAT + l
+    other = 1 - p
+    tokens = rows * TOK
+    has_left, has_right = t > 0, t < TOK - 1
+    my_cols = pl.ds(pl.multiple_of(p * half, half), half)
+    other_cols = pl.ds(pl.multiple_of(other * half, half), half)
+    fc = l * PAIR + p
+
+    peers = []
+    for o in range(1, group):
+        q = lax.rem(j + o, group)
+        peers.append((q, q // LAT, lax.rem(q, LAT)))
+
+    local = [
+        pltpu.make_async_copy(residual.at[:, my_cols], win.at[p], local_sem.at[0]),
+        pltpu.make_async_copy(grad.at[:, my_cols], grad_all.at[t], local_sem.at[1]),
+        pltpu.make_async_copy(encoder, enc_v, local_sem.at[2]),
+        pltpu.make_async_copy(decoder, dec_v, local_sem.at[3]),
+    ]
+    for copy in local:
+        copy.start()
+
+    barrier = pltpu.get_barrier_semaphore()
+    for _, qp, ql in peers:
+        pl.semaphore_signal(barrier, inc=1, device_id=(qp, ql, t), device_id_type=MESH)
+    for there, where in ((has_left, t - 1), (has_right, t + 1)):
+        @pl.when(there)
+        def _():
+            for c in range(PAIR):
+                pl.semaphore_signal(barrier, inc=1, device_id=(c, l, where), device_id_type=MESH)
+    sides = jnp.where(has_left, 1, 0) + jnp.where(has_right, 1, 0)
+    pl.semaphore_wait(barrier, group - 1 + PAIR * sides)
+
+    match_all[p * 2] = matches[...]
+    m_partner = remote(
+        matches, match_all.at[p * 2], match_send.at[0], match_recv.at[p, 0], (other, l, t)
+    )
+    m_partner.start()
+    m_left = [
+        remote(matches, match_all.at[p * 2 + 1], match_send.at[1 + c], match_recv.at[p, 1], (c, l, t - 1))
+        for c in range(PAIR)
+    ]
+
+    @pl.when(has_left)
+    def _():
+        for copy in m_left:
+            copy.start()
+
+    w_copy = remote(residual.at[:, other_cols], win.at[p], win_sem.at[0], win_sem.at[1], (other, l, t))
+    w_copy.start()
+
+    g_right = remote(grad.at[:, my_cols], grad_all.at[t], grad_send.at[t, 0], grad_recv.at[t], (p, l, t + 1))
+    g_left = remote(grad.at[:, my_cols], grad_all.at[t], grad_send.at[t, 1], grad_recv.at[t], (p, l, t - 1))
+
+    @pl.when(has_right)
+    def _():
+        g_right.start()
+
+    @pl.when(has_left)
+    def _():
+        g_left.start()
+
+    n_sel = group * SLOT_ROWS
+    r_id = lax.broadcasted_iota(jnp.int32, (n_sel, rows), 0)
+    c_id = lax.broadcasted_iota(jnp.int32, (n_sel, rows), 1)
+    block_of = (r_id // SLOT_ROWS) * TOK + t
+    slot_of = lax.rem(r_id // TBLK, MOST).astype(F32)
+    same_row = lax.rem(r_id, TBLK) == lax.rem(c_id, TBLK)
+    u_r = lax.broadcasted_iota(jnp.int32, (rows, rows), 0)
+    u_c = lax.broadcasted_iota(jnp.int32, (rows, rows), 1)
+    before = jnp.where((u_r // TBLK < u_c // TBLK) & (lax.rem(u_r, TBLK) == 0), 1.0, 0.0).astype(BF16)
+    for s in range(TOK):
+        listed = jnp.zeros((n_sel, rows), F32)
+        for a in range(act.shape[0]):
+            listed = listed + jnp.where(act[a : a + 1, s * rows : (s + 1) * rows] == block_of, 1.0, 0.0)
+        rank = jnp.dot(listed.astype(BF16), before, preferred_element_type=F32)
+        choose[s] = jnp.where(same_row & (rank == slot_of), listed, 0.0).astype(BF16)
+
+    m_recv = remote(matches, match_all.at[other * 2], match_send.at[0], match_recv.at[other, 0], (other, l, t))
+    m_recv.wait_recv()
+    local[0].wait()
+    w_recv = remote(residual.at[:, other_cols], win.at[other], win_sem.at[0], win_sem.at[1], (other, l, t))
+    w_recv.wait_recv()
+    row_id = lax.broadcasted_iota(jnp.int32, (rows, rows), 0) + t * rows
+
+    def matched(which):
+        total = None
+        for model, sign in ((0, -1.0), (1, 1.0)):
+            hit = jnp.where(match_all[model * 2 + which] == row_id, sign, 0.0)
+            term = jnp.dot(hit.T.astype(BF16), win[model], preferred_element_type=F32)
+            total = term if total is None else total + term
+        return total
+
+    p_copy = remote(part_out, part_in, part_sem.at[0], part_sem.at[1], (p, l, t + 1))
+
+    @pl.when(has_right)
+    def _():
+        for model in range(2):
+            remote(
+                matches, match_all.at[model * 2 + 1], match_send.at[0], match_recv.at[model, 1], (other, l, t)
+            ).wait_recv()
+        part_out[...] = matched(1).astype(BF16)
+        p_copy.start()
+
+    own_delta[...] = matched(0)
+
+    @pl.when(has_left)
+    def _():
+        p_copy.wait_recv()
+        own_delta[...] += part_in[...].astype(F32)
+
+    delta_all[t] = own_delta[...].astype(BF16)
+
+    def pass_on(buf, send, recv, s, i):
+        right = remote(buf.at[s], buf.at[s], send.at[s, 0], recv.at[s], (p, l, t + 1))
+        left = remote(buf.at[s], buf.at[s], send.at[s, 1], recv.at[s], (p, l, t - 1))
+        return right, left
+
+    def order(i):
+        m = jnp.minimum(t, TOK - 1 - t)
+        d = (i + 1) // 2
+        near = jnp.where(lax.rem(i, 2) == 1, t - d, t + d)
+        far = jnp.where(t < TOK - 1 - t, t + (i - m), t - (i - m))
+        return jnp.where(i <= 2 * m, near, far)
+
+    def spread(i, buf, send, recv, sent, got, s_send, s_recv, first):
+        s = order(i)
+        right, left = pass_on(buf, send, recv, s, i)
+
+        @pl.when(i > 0)
+        def _():
+            right.wait_recv()
+
+        own_goes = 0 if first else 1
+
+        @pl.when(has_right & (s + own_goes <= t))
+        def _():
+            right.start()
+
+        @pl.when(has_left & (s - own_goes >= t))
+        def _():
+            left.start()
+
+        sent[s] = (
+            jnp.dot(choose[s], buf[s], preferred_element_type=F32)
+            .astype(BF16)
+            .reshape(group, SLOT_ROWS, half)
+        )
+        for q, qp, ql in peers:
+            remote(sent.at[s, q], got.at[fc, s], s_send.at[s, q], s_recv.at[fc, s], (qp, ql, t)).start()
+        got[fc, s] = sent[s, j]
+
+    def spread_delta(i, carry):
+        spread(i, delta_all, delta_send, delta_recv, sent_delta, got_delta, sd_send, sd_recv, True)
+        return carry
+
+    def arrive(got, s_recv, s):
+        for q, qp, ql in peers:
+            qf = ql * PAIR + qp
+            remote(got.at[qf, s], got.at[qf, s], s_recv.at[qf, s], s_recv.at[qf, s], (qp, ql, t)).wait_recv()
+
+    def encode(i, carry):
+        s = order(i)
+        arrive(got_delta, sd_recv, s)
+        pre = jnp.zeros((SLOT_ROWS, enc_v.shape[1]), F32)
+        for c in range(group):
+            pre = pre + jnp.dot(
+                got_delta[c, s], enc_v[c * half : (c + 1) * half, :], preferred_element_type=F32
+            )
+        firing = jnp.maximum(pre + enc_bias[...], 0.0)
+        fire[s] = firing
+        lean = firing.astype(BF16)
+        for c in range(group):
+            pieces[s, c] = jnp.dot(
+                lean, dec_v[:, c * half : (c + 1) * half], preferred_element_type=F32
+            ).astype(BF16)
+        for q, qp, ql in peers:
+            remote(
+                pieces.at[s, ql * PAIR + qp], back.at[s, j], pc_send.at[s, q], pc_recv.at[s, j], (qp, ql, t)
+            ).start()
+        back[s, j] = pieces[s, fc]
+        return carry
+
+    def spread_grad(i, carry):
+        spread(i, grad_all, grad_send, grad_recv, sent_grad, got_grad, sg_send, sg_recv, False)
+        return carry
+
+    def first_loop(i, carry):
+        spread_delta(i, 0)
+        spread_grad(i, 0)
+        return carry
+
+    local[1].wait()
+    lax.fori_loop(0, TOK, first_loop, 0)
+    local[2].wait()
+    local[3].wait()
+    lax.fori_loop(0, TOK, encode, 0)
+
+    def combine(k, carry):
+        s = order(TOK - 1 - k)
+        for q, qp, ql in peers:
+            remote(back.at[s, q], back.at[s, q], pc_recv.at[s, q], pc_recv.at[s, q], (qp, ql, t)).wait_recv()
+        put = choose[s].astype(F32).T.astype(BF16)
+        own_delta[...] = jnp.dot(put, back[s].reshape(n_sel, half), preferred_element_type=F32)
+
+        def add_from(side):
+            remote(
+                sum_out.at[s], sum_in.at[side, s], sum_send.at[s], sum_recv.at[side, s], (p, l, t)
+            ).wait_recv()
+            own_delta[...] += sum_in[side, s].astype(F32)
+
+        @pl.when(has_left & (s >= t))
+        def _():
+            add_from(0)
+
+        @pl.when(has_right & (s <= t))
+        def _():
+            add_from(1)
+
+        @pl.when(s != t)
+        def _():
+            sum_out[s] = own_delta[...].astype(BF16)
+
+        @pl.when(s > t)
+        def _():
+            remote(sum_out.at[s], sum_in.at[0, s], sum_send.at[s], sum_recv.at[0, s], (p, l, t + 1)).start()
+
+        @pl.when(s < t)
+        def _():
+            remote(sum_out.at[s], sum_in.at[1, s], sum_send.at[s], sum_recv.at[1, s], (p, l, t - 1)).start()
+
+        return carry
+
+    lax.fori_loop(0, TOK, combine, 0)
+    out[:, my_cols] = (own_delta[...] + dec_bias[:, my_cols]).astype(BF16)
+    o_copy = remote(out.at[:, my_cols], out.at[:, my_cols], out_sem.at[0], out_sem.at[1], (other, l, t))
+    o_copy.start()
+
+    def arrive_grad(s, carry):
+        arrive(got_grad, sg_recv, s)
+        return carry
+
+    lax.fori_loop(0, TOK, arrive_grad, 0)
+    inner = jnp.zeros((TOK * SLOT_ROWS, enc_v.shape[1]), F32)
+    for c in range(group):
+        inner = inner + lax.dot_general(
+            got_grad[c].reshape(TOK * SLOT_ROWS, half),
+            dec_v[:, c * half : (c + 1) * half],
+            (((1,), (1,)), ((), ())),
+            preferred_element_type=F32,
+        )
+    total = jnp.zeros((1, enc_v.shape[1]), F32)
+    heads = lax.rem(lax.broadcasted_iota(jnp.int32, (1, rows), 1), TBLK) == 0
+    slot = (lax.broadcasted_iota(jnp.int32, (SLOT_ROWS, 1), 0) // TBLK).astype(F32)
+    for s in range(TOK):
+        mine = jnp.zeros((1, rows), F32)
+        for a in range(act.shape[0]):
+            mine = mine + jnp.where(act[a : a + 1, s * rows : (s + 1) * rows] == j * TOK + t, 1.0, 0.0)
+        count = jnp.sum(jnp.where(heads, mine, 0.0), axis=1, keepdims=True)
+        used = jnp.where(slot < count, fire[s], 0.0)
+        total = total + jnp.sum(
+            used * inner[s * SLOT_ROWS : (s + 1) * SLOT_ROWS], axis=0, keepdims=True
+        )
+    scores[...] = total / math.sqrt(tokens / TBLK)
+
+    m_partner.wait_send()
+    w_copy.wait_send()
+
+    @pl.when(has_left)
+    def _():
+        for copy in m_left:
+            copy.wait_send()
+
+    @pl.when(has_right)
+    def _():
+        p_copy.wait_send()
+
+    def drain(s, carry):
+        for buf, send, recv in ((delta_all, delta_send, delta_recv), (grad_all, grad_send, grad_recv)):
+            right, left = pass_on(buf, send, recv, s, 0)
+
+            @pl.when(has_right & (s <= t))
+            def _():
+                right.wait_send()
+
+            @pl.when(has_left & (s >= t))
+            def _():
+                left.wait_send()
+
+        for q, qp, ql in peers:
+            remote(sent_delta.at[s, q], got_delta.at[fc, s], sd_send.at[s, q], sd_recv.at[fc, s], (qp, ql, t)).wait_send()
+            remote(sent_grad.at[s, q], got_grad.at[fc, s], sg_send.at[s, q], sg_recv.at[fc, s], (qp, ql, t)).wait_send()
+            remote(pieces.at[s, q], back.at[s, j], pc_send.at[s, q], pc_recv.at[s, j], (qp, ql, t)).wait_send()
+
+        @pl.when(s != t)
+        def _():
+            remote(sum_out.at[s], sum_in.at[0, s], sum_send.at[s], sum_recv.at[0, s], (p, l, t)).wait_send()
+
+        return carry
+
+    lax.fori_loop(0, TOK, drain, 0)
+    o_copy.wait_send()
+    remote(out.at[:, other_cols], out.at[:, other_cols], out_sem.at[0], out_sem.at[1], (other, l, t)).wait_recv()
+
+
+def fused(
+    residual, matches, kl_grad, active_blocks, encoder, encoder_offset_bias, decoder, dec_bias
+):
+    pair, lat, tok = (lax.axis_size(a) for a in ("pair", "lat", "tok"))
+    _, rows, width = residual.shape
+    half = width // pair
+    group = pair * lat
+    lats = encoder.shape[1]
+    depth = encoder.shape[0]
+    act = jnp.repeat(active_blocks.T, TBLK, axis=1)
+    vmem = pl.BlockSpec(memory_space=pltpu.VMEM)
+    hbm = pl.BlockSpec(memory_space=pl.ANY)
+    dma = pltpu.SemaphoreType.DMA
+    slots = (SLOT_ROWS, half)
+    recon, scores = pl.pallas_call(
+        functools.partial(kernel, pair, lat, tok),
+        out_shape=(
+            jax.ShapeDtypeStruct((rows, width), BF16),
+            jax.ShapeDtypeStruct((1, lats), F32),
+        ),
+        in_specs=[hbm, vmem, hbm, vmem, hbm, vmem, hbm, vmem],
+        out_specs=(vmem, vmem),
+        scratch_shapes=[
+            pltpu.VMEM((2, rows, half), BF16),
+            pltpu.VMEM((4, 1, rows), jnp.int32),
+            pltpu.VMEM((rows, half), BF16),
+            pltpu.VMEM((rows, half), BF16),
+            pltpu.VMEM((rows, half), F32),
+            pltpu.VMEM((tok, rows, half), BF16),
+            pltpu.VMEM((tok, rows, half), BF16),
+            pltpu.VMEM((tok, group * SLOT_ROWS, rows), BF16),
+            pltpu.VMEM((tok, group) + slots, BF16),
+            pltpu.VMEM((tok, group) + slots, BF16),
+            pltpu.VMEM((group, tok) + slots, BF16),
+            pltpu.VMEM((group, tok) + slots, BF16),
+            pltpu.VMEM((tok, SLOT_ROWS, lats), F32),
+            pltpu.VMEM((tok, group) + slots, BF16),
+            pltpu.VMEM((tok, group) + slots, BF16),
+            pltpu.VMEM((tok, rows, half), BF16),
+            pltpu.VMEM((2, tok, rows, half), BF16),
+            pltpu.VMEM((depth, lats), BF16),
+            pltpu.VMEM((lats, depth), BF16),
+            dma((4,)),
+            dma((2,)),
+            dma((3,)),
+            dma((2, 2)),
+            dma((2,)),
+            dma((tok, 2)),
+            dma((tok,)),
+            dma((tok, 2)),
+            dma((tok,)),
+            dma((tok, group)),
+            dma((group, tok)),
+            dma((tok, group)),
+            dma((group, tok)),
+            dma((tok, group)),
+            dma((tok, group)),
+            dma((tok,)),
+            dma((2, tok)),
+            dma((2,)),
+        ],
+        compiler_params=pltpu.CompilerParams(
+            collective_id=0, has_side_effects=True, vmem_limit_bytes=40 * 1024 * 1024
+        ),
+    )(
+        residual[0],
+        matches,
+        kl_grad,
+        act,
+        encoder,
+        encoder_offset_bias[None],
+        decoder,
+        dec_bias[None],
+    )
+    return recon, scores[0]
+
+
 def solution(mesh):
     placed = (
         P("pair", "tok", "lat"),
@@ -112,8 +572,16 @@
         P(("pair", "lat", "tok"), None),
         P("lat"),
     )
+
+
+    def body(*args):
+        residual = args[0]
+        half = residual.shape[2] // mesh.shape["pair"]
+        fits = mesh.shape["pair"] == 2 and residual.shape[2] % 2 == 0 and half % 128 == 0
+        return (fused if fits else shards)(*args)
+
     return jax.shard_map(
-        shards,
+        body,
         mesh=mesh,
         in_specs=placed,
         out_specs=(P("tok", "lat"), P(("pair", "lat", "tok"))),

time: 149 us -> 62.7 us (0.42)
  waiting for transfers between devices: 86.7 us -> 0 us
  Pallas kernels: 0 us -> 54.3 us
  blocking collectives: 16.4 us -> 0 us
  starting transfers between devices: 13.4 us -> 0 us
  between operations: 13.9 us -> 0.68 us
  matrix products: 6.75 us -> 0 us
  other arithmetic: 5.9 us -> 0 us
    pallas_call x0 -> x1, Pallas kernels: none -> 54.3 us  [fused(): pl.pallas_call(functools.partial(kernel, pair, lat, tok), out_shape=(jax....]
    all_gather x2 -> x0, waiting for transfers between devices: 28.2 us -> none  [the longest x1 28.2 us: shards(): lax.all_gather(delta_rows, 'lat', axis=1, tiled=True)]
    psum x1 -> x0, waiting for transfers between devices: 19.4 us -> none  [shards(): summed = lax.psum(shared, 'pair').astype(jnp.float32)]
    reduce_scatter x1 -> x0, waiting for transfers between devices: 19.1 us -> none  [shards(): lax.psum_scatter(source_sums.astype(jnp.bfloat16), 'lat', scatter_dimensi...]
    all_to_all x1 -> x0, blocking collectives: 16.4 us -> none  [shards(): lax.all_to_all(pieces_out, 'tok', split_axis=0, concat_axis=0, tiled=True)]
    all_to_all x2 -> x0, waiting for transfers between devices: 13.2 us -> none  [the longest x1 13.2 us: shards(): lax.all_to_all(sent_delta, 'tok', split_axis=0, concat_axis=0, tiled=True)]
    all_to_all x2 -> x0, starting transfers between devices: 8.07 us -> none  [the longest x1 4.6 us: shards(): lax.all_to_all(sent_delta, 'tok', split_axis=0, concat_axis=0, tiled=True)]
    unnamed x10 -> x18, local copies, waits for them, and re-layouts: 0.03 us -> 6.82 us
  transfers between devices with their start and end apart: 8 -> 0, of which waited for: 6 -> 0; matrix products, arithmetic and copies ran while one was open for 7% -> 0% of each run, Pallas kernels for 0% -> 0%
where the time goes in v1:
time: 62.7 us; the launch traced here: 61.9 us
  Pallas kernels  54.3 us (87%)
  local copies, waits for them, and re-layouts  6.99 us (11%)
  between operations  0.68 us (1%)
    pallas_call x1, Pallas kernels, fused(): pl.pallas_call(functools.partial(kernel, pair, lat, tok), out_shape=(jax....  54.3 us
    unnamed x18, local copies, waits for them, and re-layouts  6.82 us

profile of v1, /device:TPU:0, one launch (start us, length us, event | category | flops | bytes accessed | tf_op | source)
XLA Modules:
  0.0 61.9 jit_solution(1202930518746923996)
XLA Ops:
  0.6 0.0 copy-start.7
  0.6 0.7 %copy-done.7 = s32[64,2]{0,1:T(2,128)S(1)} copy-done((s32[64,2]{0,1:T(2,128)S(1)}, s32[64,2]{0,1:T(2,128)}, u32[]{:S(2)}) %copy-start.7) | copy-done | bytes 536
  1.3 0.1 broadcast_in_dim.9
  1.4 0.0 copy-start.4
  1.4 0.0 copy-start.5
  1.4 0.0 copy-start.6
  1.4 0.1 reshape.7.act
  1.5 0.6 copy-done.4
  2.1 0.0 copy-done.5
  2.1 0.0 copy-done.6
  2.1 0.0 copy-start
  2.1 1.2 %copy-done = bf16[4096,128]{1,0:T(8,128)(2,1)S(1)} copy-done((bf16[4096,128]{1,0:T(8,128)(2,1)S(1)}, bf16[4096,128]{1,0:T(8,128)(2,1)}, u32[]{:S(2)}) %copy-start) | copy-done | bytes 1048600
  3.3 0.0 copy-start.1
  3.3 1.2 %copy-done.1 = bf16[128,4096]{1,0:T(8,128)(2,1)S(1)} copy-done((bf16[128,4096]{1,0:T(8,128)(2,1)S(1)}, bf16[128,4096]{1,0:T(8,128)(2,1)}, u32[]{:S(2)}) %copy-start.1) | copy-done | bytes 1048600
  4.5 0.0 copy-start.2
  4.5 0.9 %copy-done.2 = bf16[1,128,1024]{2,1,0:T(8,128)(2,1)S(1)} copy-done((bf16[1,128,1024]{2,1,0:T(8,128)(2,1)S(1)}, bf16[1,128,1024]{2,1,0:T(8,128)(2,1)}, u32[]{:S(2)}) %copy-start.2) | copy-done | bytes 262168
  5.5 0.0 copy-start.3
  5.5 0.9 %copy-done.3 = bf16[128,1024]{1,0:T(8,128)(2,1)S(1)} copy-done((bf16[128,1024]{1,0:T(8,128)(2,1)S(1)}, bf16[128,1024]{1,0:T(8,128)(2,1)}, u32[]{:S(2)}) %copy-start.3) | copy-done | bytes 262168
  6.4 54.3 %shard_map.95 = (bf16[128,1024]{1,0:T(8,128)(2,1)S(1)}, f32[1,128]{1,0:T(1,128)S(1)}) custom-call(bf16[128,1024]{1,0:T(8,128)(2,1)S(1)} %bitcast.5, s32[1,128]{1,0:T(1,128)S(1)} %copy-done.5, bf16[128,1024]{1,0:T(8,128)(2,1)S(1)} %copy-done.3, s32[2,512]{1,0:T(2,128)S(1)} %reshape.7.act, bf16[4096,128]{1,0:T(8,128)(2,1)S(1)} %copy-done, ...), custom_call_target="tpu_custom_call" | custom-call | tf_op jit(solution)/shard_map/pallas_call | solution.py:501
  60.7 0.7 %copy.12 = bf16[128,1024]{1,0:T(8,128)(2,1)} copy(bf16[128,1024]{1,0:T(8,128)(2,1)S(1)} %get-tuple-element.8) | data formatting | bytes 524288
  61.4 0.5 copy.13
Async XLA Ops:
  0.6 0.7 %copy-start.7 = (s32[64,2]{0,1:T(2,128)S(1)}, s32[64,2]{0,1:T(2,128)}, u32[]{:S(2)}) copy-start(s32[64,2]{0,1:T(2,128)} %param.11) | copy-start | bytes 1540
  1.4 0.7 %copy-start.4 = (f32[1024]{0:T(1024)S(1)}, f32[1024]{0:T(1024)}, u32[]{:S(2)}) copy-start(f32[1024]{0:T(1024)} %param.15) | copy-start | bytes 12292
  1.4 0.7 %copy-start.5 = (s32[1,128]{1,0:T(1,128)S(1)}, s32[1,128]{1,0:T(1,128)}, u32[]{:S(2)}) copy-start(s32[1,128]{1,0:T(1,128)} %matches.1) | copy-start | bytes 1540
  1.4 0.7 %copy-start.6 = (f32[128]{0:T(128)S(1)}, f32[128]{0:T(128)}, u32[]{:S(2)}) copy-start(f32[128]{0:T(128)} %param.13) | copy-start | bytes 1540
  2.1 1.2 %copy-start = (bf16[4096,128]{1,0:T(8,128)(2,1)S(1)}, bf16[4096,128]{1,0:T(8,128)(2,1)}, u32[]{:S(2)}) copy-start(bf16[4096,128]{1,0:T(8,128)(2,1)} %encoder.1) | copy-start | bytes 3145732
  3.3 1.2 %copy-start.1 = (bf16[128,4096]{1,0:T(8,128)(2,1)S(1)}, bf16[128,4096]{1,0:T(8,128)(2,1)}, u32[]{:S(2)}) copy-start(bf16[128,4096]{1,0:T(8,128)(2,1)} %decoder.1) | copy-start | bytes 3145732
  4.5 0.9 %copy-start.2 = (bf16[1,128,1024]{2,1,0:T(8,128)(2,1)S(1)}, bf16[1,128,1024]{2,1,0:T(8,128)(2,1)}, u32[]{:S(2)}) copy-start(bf16[1,128,1024]{2,1,0:T(8,128)(2,1)} %param.8) | copy-start | bytes 786436
  5.5 0.9 %copy-start.3 = (bf16[128,1024]{1,0:T(8,128)(2,1)S(1)}, bf16[128,1024]{1,0:T(8,128)(2,1)}, u32[]{:S(2)}) copy-start(bf16[128,1024]{1,0:T(8,128)(2,1)} %grad.1) | copy-start | bytes 786436

commit v2 on v1

--- a/solution.py
+++ b/solution.py
@@ -143,6 +143,7 @@
     delta_all,
     grad_all,
     choose,
+    put,
     sent_delta,
     sent_grad,
     got_delta,
@@ -204,43 +205,14 @@
     barrier = pltpu.get_barrier_semaphore()
     for _, qp, ql in peers:
         pl.semaphore_signal(barrier, inc=1, device_id=(qp, ql, t), device_id_type=MESH)
-    for there, where in ((has_left, t - 1), (has_right, t + 1)):
-        @pl.when(there)
-        def _():
-            for c in range(PAIR):
-                pl.semaphore_signal(barrier, inc=1, device_id=(c, l, where), device_id_type=MESH)
-    sides = jnp.where(has_left, 1, 0) + jnp.where(has_right, 1, 0)
-    pl.semaphore_wait(barrier, group - 1 + PAIR * sides)
-
-    match_all[p * 2] = matches[...]
-    m_partner = remote(
-        matches, match_all.at[p * 2], match_send.at[0], match_recv.at[p, 0], (other, l, t)
-    )
-    m_partner.start()
-    m_left = [
-        remote(matches, match_all.at[p * 2 + 1], match_send.at[1 + c], match_recv.at[p, 1], (c, l, t - 1))
-        for c in range(PAIR)
-    ]
-
-    @pl.when(has_left)
-    def _():
-        for copy in m_left:
-            copy.start()
-
-    w_copy = remote(residual.at[:, other_cols], win.at[p], win_sem.at[0], win_sem.at[1], (other, l, t))
-    w_copy.start()
-
-    g_right = remote(grad.at[:, my_cols], grad_all.at[t], grad_send.at[t, 0], grad_recv.at[t], (p, l, t + 1))
-    g_left = remote(grad.at[:, my_cols], grad_all.at[t], grad_send.at[t, 1], grad_recv.at[t], (p, l, t - 1))
-
-    @pl.when(has_right)
-    def _():
-        g_right.start()
-
-    @pl.when(has_left)
-    def _():
-        g_left.start()
-
+    for where in range(TOK):
+        @pl.when(t != where)
+        def _():
+            pl.semaphore_signal(barrier, inc=1, device_id=(p, l, where), device_id_type=MESH)
+
+        @pl.when((where == t - 1) | (where == t + 1))
+        def _():
+            pl.semaphore_signal(barrier, inc=1, device_id=(other, l, where), device_id_type=MESH)
     n_sel = group * SLOT_ROWS
     r_id = lax.broadcasted_iota(jnp.int32, (n_sel, rows), 0)
     c_id = lax.broadcasted_iota(jnp.int32, (n_sel, rows), 1)
@@ -255,44 +227,43 @@
         for a in range(act.shape[0]):
             listed = listed + jnp.where(act[a : a + 1, s * rows : (s + 1) * rows] == block_of, 1.0, 0.0)
         rank = jnp.dot(listed.astype(BF16), before, preferred_element_type=F32)
-        choose[s] = jnp.where(same_row & (rank == slot_of), listed, 0.0).astype(BF16)
-
-    m_recv = remote(matches, match_all.at[other * 2], match_send.at[0], match_recv.at[other, 0], (other, l, t))
-    m_recv.wait_recv()
-    local[0].wait()
-    w_recv = remote(residual.at[:, other_cols], win.at[other], win_sem.at[0], win_sem.at[1], (other, l, t))
-    w_recv.wait_recv()
-    row_id = lax.broadcasted_iota(jnp.int32, (rows, rows), 0) + t * rows
-
-    def matched(which):
-        total = None
-        for model, sign in ((0, -1.0), (1, 1.0)):
-            hit = jnp.where(match_all[model * 2 + which] == row_id, sign, 0.0)
-            term = jnp.dot(hit.T.astype(BF16), win[model], preferred_element_type=F32)
-            total = term if total is None else total + term
-        return total
-
-    p_copy = remote(part_out, part_in, part_sem.at[0], part_sem.at[1], (p, l, t + 1))
+        chosen = jnp.where(same_row & (rank == slot_of), listed, 0.0)
+        choose[s] = chosen.astype(BF16)
+        put[s] = chosen.T.astype(BF16)
+
+    sides = jnp.where(has_left, 1, 0) + jnp.where(has_right, 1, 0)
+    pl.semaphore_wait(barrier, group - 1 + TOK - 1 + sides)
+
+    match_all[p * 2] = matches[...]
+    m_partner = remote(
+        matches, match_all.at[p * 2], match_send.at[0], match_recv.at[p, 0], (other, l, t)
+    )
+    m_partner.start()
+    m_left = [
+        remote(matches, match_all.at[p * 2 + 1], match_send.at[1 + c], match_recv.at[p, 1], (c, l, t - 1))
+        for c in range(PAIR)
+    ]
+
+    @pl.when(has_left)
+    def _():
+        for copy in m_left:
+            copy.start()
+
+    w_copy = remote(residual.at[:, other_cols], win.at[p], win_sem.at[0], win_sem.at[1], (other, l, t))
+    w_copy.start()
+
+    g_right = remote(grad.at[:, my_cols], grad_all.at[t], grad_send.at[t, 0], grad_recv.at[t], (p, l, t + 1))
+    g_left = remote(grad.at[:, my_cols], grad_all.at[t], grad_send.at[t, 1], grad_recv.at[t], (p, l, t - 1))
 
     @pl.when(has_right)
     def _():
-        for model in range(2):
-            remote(
-                matches, match_all.at[model * 2 + 1], match_send.at[0], match_recv.at[model, 1], (other, l, t)
-            ).wait_recv()
-        part_out[...] = matched(1).astype(BF16)
-        p_copy.start()
-
-    own_delta[...] = matched(0)
+        g_right.start()
 
     @pl.when(has_left)
     def _():
-        p_copy.wait_recv()
-        own_delta[...] += part_in[...].astype(F32)
-
-    delta_all[t] = own_delta[...].astype(BF16)
-
-    def pass_on(buf, send, recv, s, i):
+        g_left.start()
+
+    def pass_on(buf, send, recv, s):
         right = remote(buf.at[s], buf.at[s], send.at[s, 0], recv.at[s], (p, l, t + 1))
         left = remote(buf.at[s], buf.at[s], send.at[s, 1], recv.at[s], (p, l, t - 1))
         return right, left
@@ -306,9 +277,9 @@
 
     def spread(i, buf, send, recv, sent, got, s_send, s_recv, first):
         s = order(i)
-        right, left = pass_on(buf, send, recv, s, i)
-
-        @pl.when(i > 0)
+        right, left = pass_on(buf, send, recv, s)
+
+        @pl.when(s != t)
         def _():
             right.wait_recv()
 
@@ -331,16 +302,15 @@
             remote(sent.at[s, q], got.at[fc, s], s_send.at[s, q], s_recv.at[fc, s], (qp, ql, t)).start()
         got[fc, s] = sent[s, j]
 
-    def spread_delta(i, carry):
+    def spread_delta(i):
         spread(i, delta_all, delta_send, delta_recv, sent_delta, got_delta, sd_send, sd_recv, True)
-        return carry
 
     def arrive(got, s_recv, s):
         for q, qp, ql in peers:
             qf = ql * PAIR + qp
             remote(got.at[qf, s], got.at[qf, s], s_recv.at[qf, s], s_recv.at[qf, s], (qp, ql, t)).wait_recv()
 
-    def encode(i, carry):
+    def encode(i):
         s = order(i)
         arrive(got_delta, sd_recv, s)
         pre = jnp.zeros((SLOT_ROWS, enc_v.shape[1]), F32)
@@ -360,62 +330,85 @@
                 pieces.at[s, ql * PAIR + qp], back.at[s, j], pc_send.at[s, q], pc_recv.at[s, j], (qp, ql, t)
             ).start()
         back[s, j] = pieces[s, fc]
-        return carry
-
-    def spread_grad(i, carry):
+
+    def spread_grad(i):
         spread(i, grad_all, grad_send, grad_recv, sent_grad, got_grad, sg_send, sg_recv, False)
-        return carry
-
-    def first_loop(i, carry):
-        spread_delta(i, 0)
-        spread_grad(i, 0)
-        return carry
 
     local[1].wait()
-    lax.fori_loop(0, TOK, first_loop, 0)
+    spread_grad(0)
+    m_recv = remote(matches, match_all.at[other * 2], match_send.at[0], match_recv.at[other, 0], (other, l, t))
+    m_recv.wait_recv()
+    local[0].wait()
+    w_recv = remote(residual.at[:, other_cols], win.at[other], win_sem.at[0], win_sem.at[1], (other, l, t))
+    w_recv.wait_recv()
+    row_id = lax.broadcasted_iota(jnp.int32, (rows, rows), 0) + t * rows
+
+    def matched(which):
+        total = None
+        for model, sign in ((0, -1.0), (1, 1.0)):
+            hit = jnp.where(match_all[model * 2 + which] == row_id, sign, 0.0)
+            term = jnp.dot(hit.T.astype(BF16), win[model], preferred_element_type=F32)
+            total = term if total is None else total + term
+        return total
+
+    p_copy = remote(part_out, part_in, part_sem.at[0], part_sem.at[1], (p, l, t + 1))
+
+    @pl.when(has_right)
+    def _():
+        for model in range(2):
+            remote(
+                matches, match_all.at[model * 2 + 1], match_send.at[0], match_recv.at[model, 1], (other, l, t)
+            ).wait_recv()
+        part_out[...] = matched(1).astype(BF16)
+        p_copy.start()
+
+    own_delta[...] = matched(0)
+    if TOK > 1:
+        spread_grad(1)
+
+    @pl.when(has_left)
+    def _():
+        p_copy.wait_recv()
+        own_delta[...] += part_in[...].astype(F32)
+
+    delta_all[t] = own_delta[...].astype(BF16)
+
+    def place(i):
+        s = order(i)
+        for q, qp, ql in peers:
+            remote(back.at[s, q], back.at[s, q], pc_recv.at[s, q], pc_recv.at[s, q], (qp, ql, t)).wait_recv()
+        placed = jnp.dot(put[s], back[s].reshape(n_sel, half), preferred_element_type=F32)
+
+        @pl.when(s == t)
+        def _():
+            own_delta[...] = placed
+
+        @pl.when(s != t)
+        def _():
+            sum_out[s] = placed.astype(BF16)
+            remote(sum_out.at[s], sum_in.at[t], sum_send.at[s], sum_recv.at[t], (p, l, s)).start()
+
+    spread_delta(0)
     local[2].wait()
     local[3].wait()
-    lax.fori_loop(0, TOK, encode, 0)
-
-    def combine(k, carry):
-        s = order(TOK - 1 - k)
-        for q, qp, ql in peers:
-            remote(back.at[s, q], back.at[s, q], pc_recv.at[s, q], pc_recv.at[s, q], (qp, ql, t)).wait_recv()
-        put = choose[s].astype(F32).T.astype(BF16)
-        own_delta[...] = jnp.dot(put, back[s].reshape(n_sel, half), preferred_element_type=F32)
-
-        def add_from(side):
-            remote(
-                sum_out.at[s], sum_in.at[side, s], sum_send.at[s], sum_recv.at[side, s], (p, l, t)
-            ).wait_recv()
-            own_delta[...] += sum_in[side, s].astype(F32)
-
-        @pl.when(has_left & (s >= t))
-        def _():
-            add_from(0)
-
-        @pl.when(has_right & (s <= t))
-        def _():
-            add_from(1)
-
-        @pl.when(s != t)
-        def _():
-            sum_out[s] = own_delta[...].astype(BF16)
-
-        @pl.when(s > t)
-        def _():
-            remote(sum_out.at[s], sum_in.at[0, s], sum_send.at[s], sum_recv.at[0, s], (p, l, t + 1)).start()
-
-        @pl.when(s < t)
-        def _():
-            remote(sum_out.at[s], sum_in.at[1, s], sum_send.at[s], sum_recv.at[1, s], (p, l, t - 1)).start()
+
+    def step(i, carry):
+        encode(i)
+
+        @pl.when(i + 1 < TOK)
+        def _():
+            spread_delta(i + 1)
+
+        place(i)
+
+        @pl.when(i + 2 < TOK)
+        def _():
+            spread_grad(i + 2)
 
         return carry
 
-    lax.fori_loop(0, TOK, combine, 0)
-    out[:, my_cols] = (own_delta[...] + dec_bias[:, my_cols]).astype(BF16)
-    o_copy = remote(out.at[:, my_cols], out.at[:, my_cols], out_sem.at[0], out_sem.at[1], (other, l, t))
-    o_copy.start()
+    lax.fori_loop(0, TOK - 1, step, 0)
+    encode(TOK - 1)
 
     def arrive_grad(s, carry):
         arrive(got_grad, sg_recv, s)
@@ -430,6 +423,8 @@
             (((1,), (1,)), ((), ())),
             preferred_element_type=F32,
         )
+    place(TOK - 1)
+
     total = jnp.zeros((1, enc_v.shape[1]), F32)
     heads = lax.rem(lax.broadcasted_iota(jnp.int32, (1, rows), 1), TBLK) == 0
     slot = (lax.broadcasted_iota(jnp.int32, (SLOT_ROWS, 1), 0) // TBLK).astype(F32)
@@ -444,6 +439,15 @@
         )
     scores[...] = total / math.sqrt(tokens / TBLK)
 
+    for i in range(1, TOK):
+        s = order(i)
+        remote(sum_out.at[s], sum_in.at[s], sum_send.at[s], sum_recv.at[s], (p, l, s)).wait_recv()
+        own_delta[...] += sum_in[s].astype(F32)
+
+    out[:, my_cols] = (own_delta[...] + dec_bias[:, my_cols]).astype(BF16)
+    o_copy = remote(out.at[:, my_cols], out.at[:, my_cols], out_sem.at[0], out_sem.at[1], (other, l, t))
+    o_copy.start()
+
     m_partner.wait_send()
     w_copy.wait_send()
 
@@ -458,7 +462,7 @@
 
     def drain(s, carry):
         for buf, send, recv in ((delta_all, delta_send, delta_recv), (grad_all, grad_send, grad_recv)):
-            right, left = pass_on(buf, send, recv, s, 0)
+            right, left = pass_on(buf, send, recv, s)
 
             @pl.when(has_right & (s <= t))
             def _():
@@ -475,7 +479,7 @@
 
         @pl.when(s != t)
         def _():
-            remote(sum_out.at[s], sum_in.at[0, s], sum_send.at[s], sum_recv.at[0, s], (p, l, t)).wait_send()
+            remote(sum_out.at[s], sum_in.at[t], sum_send.at[s], sum_recv.at[t], (p, l, s)).wait_send()
 
         return carry
 
@@ -495,7 +499,7 @@
     depth = encoder.shape[0]
     act = jnp.repeat(active_blocks.T, TBLK, axis=1)
     vmem = pl.BlockSpec(memory_space=pltpu.VMEM)
-    hbm = pl.BlockSpec(memory_space=pl.ANY)
+    hbm = pl.BlockSpec(memory_space=pltpu.HBM)
     dma = pltpu.SemaphoreType.DMA
     slots = (SLOT_ROWS, half)
     recon, scores = pl.pallas_call(
@@ -515,6 +519,7 @@
             pltpu.VMEM((tok, rows, half), BF16),
             pltpu.VMEM((tok, rows, half), BF16),
             pltpu.VMEM((tok, group * SLOT_ROWS, rows), BF16),
+            pltpu.VMEM((tok, rows, group * SLOT_ROWS), BF16),
             pltpu.VMEM((tok, group) + slots, BF16),
             pltpu.VMEM((tok, group) + slots, BF16),
             pltpu.VMEM((group, tok) + slots, BF16),
@@ -523,7 +528,7 @@
             pltpu.VMEM((tok, group) + slots, BF16),
             pltpu.VMEM((tok, group) + slots, BF16),
             pltpu.VMEM((tok, rows, half), BF16),
-            pltpu.VMEM((2, tok, rows, half), BF16),
+            pltpu.VMEM((tok, rows, half), BF16),
             pltpu.VMEM((depth, lats), BF16),
             pltpu.VMEM((lats, depth), BF16),
             dma((4,)),
@@ -542,7 +547,7 @@
             dma((tok, group)),
             dma((tok, group)),
             dma((tok,)),
-            dma((2, tok)),
+            dma((tok,)),
             dma((2,)),
         ],
         compiler_params=pltpu.CompilerParams(

time: 62.7 us -> 60 us (0.957)
  Pallas kernels: 54.3 us -> 52.1 us
    pallas_call x1, Pallas kernels: 54.3 us -> 52.1 us  [fused(): pl.pallas_call(functools.partial(kernel, pair, lat, tok), out_shape=(jax....]
where the time goes in v2:
time: 60 us; the launch traced here: 59.7 us
  Pallas kernels  52.1 us (87%)
  local copies, waits for them, and re-layouts  6.99 us (12%)
  between operations  0.68 us (1%)
    pallas_call x1, Pallas kernels, fused(): pl.pallas_call(functools.partial(kernel, pair, lat, tok), out_shape=(jax....  52.1 us
    unnamed x18, local copies, waits for them, and re-layouts  6.82 us

profile of v2, /device:TPU:0, one launch (start us, length us, event | category | flops | bytes accessed | tf_op | source)
XLA Modules:
  0.0 59.7 jit_solution(222659654700024814)
XLA Ops:
  0.6 0.0 copy-start.7
  0.6 0.7 %copy-done.7 = s32[64,2]{0,1:T(2,128)S(1)} copy-done((s32[64,2]{0,1:T(2,128)S(1)}, s32[64,2]{0,1:T(2,128)}, u32[]{:S(2)}) %copy-start.7) | copy-done | bytes 536
  1.3 0.1 broadcast_in_dim.9
  1.4 0.0 copy-start.4
  1.4 0.0 copy-start.5
  1.4 0.0 copy-start.6
  1.4 0.1 reshape.7.act
  1.5 0.6 copy-done.4
  2.1 0.0 copy-done.5
  2.1 0.0 copy-done.6
  2.1 0.0 copy-start
  2.1 1.2 %copy-done = bf16[4096,128]{1,0:T(8,128)(2,1)S(1)} copy-done((bf16[4096,128]{1,0:T(8,128)(2,1)S(1)}, bf16[4096,128]{1,0:T(8,128)(2,1)}, u32[]{:S(2)}) %copy-start) | copy-done | bytes 1048600
  3.3 0.0 copy-start.1
  3.3 1.2 %copy-done.1 = bf16[128,4096]{1,0:T(8,128)(2,1)S(1)} copy-done((bf16[128,4096]{1,0:T(8,128)(2,1)S(1)}, bf16[128,4096]{1,0:T(8,128)(2,1)}, u32[]{:S(2)}) %copy-start.1) | copy-done | bytes 1048600
  4.5 0.0 copy-start.2
  4.5 0.9 %copy-done.2 = bf16[1,128,1024]{2,1,0:T(8,128)(2,1)S(1)} copy-done((bf16[1,128,1024]{2,1,0:T(8,128)(2,1)S(1)}, bf16[1,128,1024]{2,1,0:T(8,128)(2,1)}, u32[]{:S(2)}) %copy-start.2) | copy-done | bytes 262168
  5.5 0.0 copy-start.3
  5.5 0.9 %copy-done.3 = bf16[128,1024]{1,0:T(8,128)(2,1)S(1)} copy-done((bf16[128,1024]{1,0:T(8,128)(2,1)S(1)}, bf16[128,1024]{1,0:T(8,128)(2,1)}, u32[]{:S(2)}) %copy-start.3) | copy-done | bytes 262168
  6.4 52.1 %shard_map.95 = (bf16[128,1024]{1,0:T(8,128)(2,1)S(1)}, f32[1,128]{1,0:T(1,128)S(1)}) custom-call(bf16[128,1024]{1,0:T(8,128)(2,1)S(1)} %bitcast.5, s32[1,128]{1,0:T(1,128)S(1)} %copy-done.5, bf16[128,1024]{1,0:T(8,128)(2,1)S(1)} %copy-done.3, s32[2,512]{1,0:T(2,128)S(1)} %reshape.7.act, bf16[4096,128]{1,0:T(8,128)(2,1)S(1)} %copy-done, ...), custom_call_target="tpu_custom_call" | custom-call | tf_op jit(solution)/shard_map/pallas_call | solution.py:505
  58.5 0.7 %copy.12 = bf16[128,1024]{1,0:T(8,128)(2,1)} copy(bf16[128,1024]{1,0:T(8,128)(2,1)S(1)} %get-tuple-element.8) | data formatting | bytes 524288
  59.2 0.5 copy.13
Async XLA Ops:
  0.6 0.7 %copy-start.7 = (s32[64,2]{0,1:T(2,128)S(1)}, s32[64,2]{0,1:T(2,128)}, u32[]{:S(2)}) copy-start(s32[64,2]{0,1:T(2,128)} %param.11) | copy-start | bytes 1540
  1.4 0.7 %copy-start.4 = (f32[1024]{0:T(1024)S(1)}, f32[1024]{0:T(1024)}, u32[]{:S(2)}) copy-start(f32[1024]{0:T(1024)} %param.15) | copy-start | bytes 12292
  1.4 0.7 %copy-start.5 = (s32[1,128]{1,0:T(1,128)S(1)}, s32[1,128]{1,0:T(1,128)}, u32[]{:S(2)}) copy-start(s32[1,128]{1,0:T(1,128)} %matches.1) | copy-start | bytes 1540
  1.4 0.7 %copy-start.6 = (f32[128]{0:T(128)S(1)}, f32[128]{0:T(128)}, u32[]{:S(2)}) copy-start(f32[128]{0:T(128)} %param.13) | copy-start | bytes 1540
  2.1 1.2 %copy-start = (bf16[4096,128]{1,0:T(8,128)(2,1)S(1)}, bf16[4096,128]{1,0:T(8,128)(2,1)}, u32[]{:S(2)}) copy-start(bf16[4096,128]{1,0:T(8,128)(2,1)} %encoder.1) | copy-start | bytes 3145732
  3.3 1.2 %copy-start.1 = (bf16[128,4096]{1,0:T(8,128)(2,1)S(1)}, bf16[128,4096]{1,0:T(8,128)(2,1)}, u32[]{:S(2)}) copy-start(bf16[128,4096]{1,0:T(8,128)(2,1)} %decoder.1) | copy-start | bytes 3145732
  4.5 0.9 %copy-start.2 = (bf16[1,128,1024]{2,1,0:T(8,128)(2,1)S(1)}, bf16[1,128,1024]{2,1,0:T(8,128)(2,1)}, u32[]{:S(2)}) copy-start(bf16[1,128,1024]{2,1,0:T(8,128)(2,1)} %param.8) | copy-start | bytes 786436
  5.5 0.9 %copy-start.3 = (bf16[128,1024]{1,0:T(8,128)(2,1)S(1)}, bf16[128,1024]{1,0:T(8,128)(2,1)}, u32[]{:S(2)}) copy-start(bf16[128,1024]{1,0:T(8,128)(2,1)} %grad.1) | copy-start | bytes 786436

commit v3 on v2

--- a/solution.py
+++ b/solution.py
@@ -140,9 +140,10 @@
     part_out,
     part_in,
     own_delta,
-    delta_all,
+    delta,
     grad_all,
     choose,
+    choose_own,
     put,
     sent_delta,
     sent_grad,
@@ -151,8 +152,6 @@
     fire,
     pieces,
     back,
-    sum_out,
-    sum_in,
     enc_v,
     dec_v,
     local_sem,
@@ -160,8 +159,6 @@
     match_send,
     match_recv,
     part_sem,
-    delta_send,
-    delta_recv,
     grad_send,
     grad_recv,
     sd_send,
@@ -170,8 +167,6 @@
     sg_recv,
     pc_send,
     pc_recv,
-    sum_send,
-    sum_recv,
     out_sem,
 ):
     p = lax.axis_index("pair")
@@ -205,34 +200,38 @@
     barrier = pltpu.get_barrier_semaphore()
     for _, qp, ql in peers:
         pl.semaphore_signal(barrier, inc=1, device_id=(qp, ql, t), device_id_type=MESH)
-    for where in range(TOK):
-        @pl.when(t != where)
-        def _():
-            pl.semaphore_signal(barrier, inc=1, device_id=(p, l, where), device_id_type=MESH)
-
-        @pl.when((where == t - 1) | (where == t + 1))
-        def _():
-            pl.semaphore_signal(barrier, inc=1, device_id=(other, l, where), device_id_type=MESH)
+    for step in range(1, TOK):
+        where = lax.rem(t + step, TOK)
+        for q in range(group):
+            pl.semaphore_signal(
+                barrier, inc=1, device_id=(q // LAT, q % LAT, where), device_id_type=MESH
+            )
+
     n_sel = group * SLOT_ROWS
     r_id = lax.broadcasted_iota(jnp.int32, (n_sel, rows), 0)
     c_id = lax.broadcasted_iota(jnp.int32, (n_sel, rows), 1)
-    block_of = (r_id // SLOT_ROWS) * TOK + t
+    first_of = (r_id // SLOT_ROWS) * TOK
     slot_of = lax.rem(r_id // TBLK, MOST).astype(F32)
     same_row = lax.rem(r_id, TBLK) == lax.rem(c_id, TBLK)
     u_r = lax.broadcasted_iota(jnp.int32, (rows, rows), 0)
     u_c = lax.broadcasted_iota(jnp.int32, (rows, rows), 1)
     before = jnp.where((u_r // TBLK < u_c // TBLK) & (lax.rem(u_r, TBLK) == 0), 1.0, 0.0).astype(BF16)
+
+    def chosen(shard, plane):
+        listed = jnp.zeros((n_sel, rows), F32)
+        cols = pl.ds(pl.multiple_of(shard * rows, rows), rows)
+        for a in range(act.shape[0]):
+            listed = listed + jnp.where(act[a : a + 1, cols] == first_of + plane, 1.0, 0.0)
+        rank = jnp.dot(listed.astype(BF16), before, preferred_element_type=F32)
+        return jnp.where(same_row & (rank == slot_of), listed, 0.0)
+
     for s in range(TOK):
-        listed = jnp.zeros((n_sel, rows), F32)
-        for a in range(act.shape[0]):
-            listed = listed + jnp.where(act[a : a + 1, s * rows : (s + 1) * rows] == block_of, 1.0, 0.0)
-        rank = jnp.dot(listed.astype(BF16), before, preferred_element_type=F32)
-        chosen = jnp.where(same_row & (rank == slot_of), listed, 0.0)
-        choose[s] = chosen.astype(BF16)
-        put[s] = chosen.T.astype(BF16)
-
-    sides = jnp.where(has_left, 1, 0) + jnp.where(has_right, 1, 0)
-    pl.semaphore_wait(barrier, group - 1 + TOK - 1 + sides)
+        choose[s] = chosen(s, t).astype(BF16)
+        own = chosen(t, s)
+        choose_own[s] = own.astype(BF16)
+        put[s] = own.T.astype(BF16)
+
+    pl.semaphore_wait(barrier, group * TOK - 1)
 
     match_all[p * 2] = matches[...]
     m_partner = remote(
@@ -302,9 +301,6 @@
             remote(sent.at[s, q], got.at[fc, s], s_send.at[s, q], s_recv.at[fc, s], (qp, ql, t)).start()
         got[fc, s] = sent[s, j]
 
-    def spread_delta(i):
-        spread(i, delta_all, delta_send, delta_recv, sent_delta, got_delta, sd_send, sd_recv, True)
-
     def arrive(got, s_recv, s):
         for q, qp, ql in peers:
             qf = ql * PAIR + qp
@@ -313,6 +309,11 @@
     def encode(i):
         s = order(i)
         arrive(got_delta, sd_recv, s)
+
+        @pl.when(s != t)
+        def _():
+            remote(got_delta.at[fc, s], got_delta.at[fc, s], sd_recv.at[fc, s], sd_recv.at[fc, s], (p, l, s)).wait_recv()
+
         pre = jnp.zeros((SLOT_ROWS, enc_v.shape[1]), F32)
         for c in range(group):
             pre = pre + jnp.dot(
@@ -327,9 +328,12 @@
             ).astype(BF16)
         for q, qp, ql in peers:
             remote(
-                pieces.at[s, ql * PAIR + qp], back.at[s, j], pc_send.at[s, q], pc_recv.at[s, j], (qp, ql, t)
+                pieces.at[s, ql * PAIR + qp], back.at[t, j], pc_send.at[s, q], pc_recv.at[t, j], (qp, ql, s)
             ).start()
-        back[s, j] = pieces[s, fc]
+
+        @pl.when(s != t)
+        def _():
+            remote(pieces.at[s, fc], back.at[t, j], pc_send.at[s, j], pc_recv.at[t, j], (p, l, s)).start()
 
     def spread_grad(i):
         spread(i, grad_all, grad_send, grad_recv, sent_grad, got_grad, sg_send, sg_recv, False)
@@ -371,44 +375,59 @@
         p_copy.wait_recv()
         own_delta[...] += part_in[...].astype(F32)
 
-    delta_all[t] = own_delta[...].astype(BF16)
-
-    def place(i):
+    delta[...] = own_delta[...].astype(BF16)
+
+    def send_delta(k, carry):
+        s = order(k)
+        sent_delta[s] = (
+            jnp.dot(choose_own[s], delta[...], preferred_element_type=F32)
+            .astype(BF16)
+            .reshape(group, SLOT_ROWS, half)
+        )
+        for q, qp, ql in peers:
+            remote(sent_delta.at[s, q], got_delta.at[fc, t], sd_send.at[s, q], sd_recv.at[fc, t], (qp, ql, s)).start()
+
+        @pl.when(s != t)
+        def _():
+            remote(sent_delta.at[s, j], got_delta.at[fc, t], sd_send.at[s, j], sd_recv.at[fc, t], (p, l, s)).start()
+
+        return carry
+
+    lax.fori_loop(0, TOK, send_delta, 0)
+    got_delta[fc, t] = sent_delta[t, j]
+    if TOK > 2:
+        spread_grad(2)
+    local[2].wait()
+    local[3].wait()
+
+    def step(i, carry):
+        encode(i)
+        return carry
+
+    lax.fori_loop(0, TOK - 1, step, 0)
+    for i in range(3, TOK):
+        spread_grad(i)
+    encode(TOK - 1)
+    back[t, j] = pieces[t, fc]
+
+    own_delta[...] = jnp.zeros_like(own_delta)
+
+    def combine(i, carry):
         s = order(i)
         for q, qp, ql in peers:
-            remote(back.at[s, q], back.at[s, q], pc_recv.at[s, q], pc_recv.at[s, q], (qp, ql, t)).wait_recv()
-        placed = jnp.dot(put[s], back[s].reshape(n_sel, half), preferred_element_type=F32)
-
-        @pl.when(s == t)
-        def _():
-            own_delta[...] = placed
+            remote(back.at[s, q], back.at[s, q], pc_recv.at[s, q], pc_recv.at[s, q], (qp, ql, s)).wait_recv()
 
         @pl.when(s != t)
         def _():
-            sum_out[s] = placed.astype(BF16)
-            remote(sum_out.at[s], sum_in.at[t], sum_send.at[s], sum_recv.at[t], (p, l, s)).start()
-
-    spread_delta(0)
-    local[2].wait()
-    local[3].wait()
-
-    def step(i, carry):
-        encode(i)
-
-        @pl.when(i + 1 < TOK)
-        def _():
-            spread_delta(i + 1)
-
-        place(i)
-
-        @pl.when(i + 2 < TOK)
-        def _():
-            spread_grad(i + 2)
-
+            remote(back.at[s, j], back.at[s, j], pc_recv.at[s, j], pc_recv.at[s, j], (p, l, s)).wait_recv()
+
+        own_delta[...] += jnp.dot(put[s], back[s].reshape(n_sel, half), preferred_element_type=F32)
         return carry
 
-    lax.fori_loop(0, TOK - 1, step, 0)
-    encode(TOK - 1)
+    lax.fori_loop(0, TOK, combine, 0)
+    out[:, my_cols] = (own_delta[...] + dec_bias[:, my_cols]).astype(BF16)
+    o_copy = remote(out.at[:, my_cols], out.at[:, my_cols], out_sem.at[0], out_sem.at[1], (other, l, t))
+    o_copy.start()
 
     def arrive_grad(s, carry):
         arrive(got_grad, sg_recv, s)
@@ -423,7 +442,6 @@
             (((1,), (1,)), ((), ())),
             preferred_element_type=F32,
         )
-    place(TOK - 1)
 
     total = jnp.zeros((1, enc_v.shape[1]), F32)
     heads = lax.rem(lax.broadcasted_iota(jnp.int32, (1, rows), 1), TBLK) == 0
@@ -439,15 +457,6 @@
         )
     scores[...] = total / math.sqrt(tokens / TBLK)
 
-    for i in range(1, TOK):
-        s = order(i)
-        remote(sum_out.at[s], sum_in.at[s], sum_send.at[s], sum_recv.at[s], (p, l, s)).wait_recv()
-        own_delta[...] += sum_in[s].astype(F32)
-
-    out[:, my_cols] = (own_delta[...] + dec_bias[:, my_cols]).astype(BF16)
-    o_copy = remote(out.at[:, my_cols], out.at[:, my_cols], out_sem.at[0], out_sem.at[1], (other, l, t))
-    o_copy.start()
-
     m_partner.wait_send()
     w_copy.wait_send()
 
@@ -461,16 +470,15 @@
         p_copy.wait_send()
 
     def drain(s, carry):
-        for buf, send, recv in ((delta_all, delta_send, delta_recv), (grad_all, grad_send, grad_recv)):
-            right, left = pass_on(buf, send, recv, s)
-
-            @pl.when(has_right & (s <= t))
-            def _():
-                right.wait_send()
-
-            @pl.when(has_left & (s >= t))
-            def _():
-                left.wait_send()
+        right, left = pass_on(grad_all, grad_send, grad_recv, s)
+
+        @pl.when(has_right & (s <= t))
+        def _():
+            right.wait_send()
+
+        @pl.when(has_left & (s >= t))
+        def _():
+            left.wait_send()
 
         for q, qp, ql in peers:
             remote(sent_delta.at[s, q], got_delta.at[fc, s], sd_send.at[s, q], sd_recv.at[fc, s], (qp, ql, t)).wait_send()
@@ -479,7 +487,8 @@
 
         @pl.when(s != t)
         def _():
-            remote(sum_out.at[s], sum_in.at[t], sum_send.at[s], sum_recv.at[t], (p, l, s)).wait_send()
+            remote(sent_delta.at[s, j], got_delta.at[fc, s], sd_send.at[s, j], sd_recv.at[fc, s], (p, l, s)).wait_send()
+            remote(pieces.at[s, j], back.at[s, j], pc_send.at[s, j], pc_recv.at[s, j], (p, l, s)).wait_send()
 
         return carry
 
@@ -516,8 +525,9 @@
             pltpu.VMEM((rows, half), BF16),
             pltpu.VMEM((rows, half), BF16),
             pltpu.VMEM((rows, half), F32),
+            pltpu.VMEM((rows, half), BF16),
             pltpu.VMEM((tok, rows, half), BF16),
-            pltpu.VMEM((tok, rows, half), BF16),
+            pltpu.VMEM((tok, group * SLOT_ROWS, rows), BF16),
             pltpu.VMEM((tok, group * SLOT_ROWS, rows), BF16),
             pltpu.VMEM((tok, rows, group * SLOT_ROWS), BF16),
             pltpu.VMEM((tok, group) + slots, BF16),
@@ -527,8 +537,6 @@
             pltpu.VMEM((tok, SLOT_ROWS, lats), F32),
             pltpu.VMEM((tok, group) + slots, BF16),
             pltpu.VMEM((tok, group) + slots, BF16),
-            pltpu.VMEM((tok, rows, half), BF16),
-            pltpu.VMEM((tok, rows, half), BF16),
             pltpu.VMEM((depth, lats), BF16),
             pltpu.VMEM((lats, depth), BF16),
             dma((4,)),
@@ -538,20 +546,16 @@
             dma((2,)),
             dma((tok, 2)),
             dma((tok,)),
-            dma((tok, 2)),
-            dma((tok,)),
             dma((tok, group)),
             dma((group, tok)),
             dma((tok, group)),
             dma((group, tok)),
             dma((tok, group)),
             dma((tok, group)),
-            dma((tok,)),
-            dma((tok,)),
             dma((2,)),
         ],
         compiler_params=pltpu.CompilerParams(
-            collective_id=0, has_side_effects=True, vmem_limit_bytes=40 * 1024 * 1024
+            collective_id=0, has_side_effects=True, vmem_limit_bytes=67_000_000
         ),
     )(
         residual[0],

time: 60 us -> 54.7 us (0.912)
  local copies, waits for them, and re-layouts: 6.99 us -> 3.63 us
  Pallas kernels: 52.1 us -> 50.2 us
    unnamed x18 -> x6, local copies, waits for them, and re-layouts: 6.82 us -> 2.86 us
    pallas_call x1, Pallas kernels: 52.1 us -> 50.2 us  [fused(): pl.pallas_call(functools.partial(kernel, pair, lat, tok), out_shape=(jax....]
    reshape x1, local copies, waits for them, and re-layouts: 0.1 us -> 0.7 us  [fused(): act = jnp.repeat(active_blocks.T, TBLK, axis=1)]
where the time goes in v3:
time: 54.7 us; the launch traced here: 54.5 us
  Pallas kernels  50.2 us (92%)
  local copies, waits for them, and re-layouts  3.63 us (7%)
  between operations  0.66 us (1%)
    pallas_call x1, Pallas kernels, fused(): pl.pallas_call(functools.partial(kernel, pair, lat, tok), out_shape=(jax....  50.2 us
    unnamed x6, local copies, waits for them, and re-layouts  2.86 us

profile of v3, /device:TPU:0, one launch (start us, length us, event | category | flops | bytes accessed | tf_op | source)
XLA Modules:
  0.0 54.5 jit_solution(5416311930646363558)
XLA Ops:
  0.6 0.0 copy-start
  0.6 0.7 %copy-done = s32[64,2]{0,1:T(2,128)S(1)} copy-done((s32[64,2]{0,1:T(2,128)S(1)}, s32[64,2]{0,1:T(2,128)}, u32[]{:S(2)}) %copy-start) | copy-done | bytes 536
  1.3 0.1 broadcast_in_dim.9
  1.4 0.7 %reshape.7.act = s32[2,512]{1,0:T(2,128)} reshape(s32[2,64,8]{2,1,0:T(8,128)S(1)} %broadcast_in_dim.9) | data formatting | bytes 8192 | tf_op jit(solution)/shard_map/reshape | solution.py:509
  2.1 50.2 %shard_map.95 = (bf16[128,1024]{1,0:T(8,128)(2,1)}, f32[1,128]{1,0:T(1,128)}) custom-call(bf16[128,1024]{1,0:T(8,128)(2,1)} %bitcast.5, s32[1,128]{1,0:T(1,128)} %matches.1, bf16[128,1024]{1,0:T(8,128)(2,1)} %grad.1, s32[2,512]{1,0:T(2,128)} %reshape.7.act, bf16[4096,128]{1,0:T(8,128)(2,1)} %encoder.1, f32[1,128]{1,0:T(1,128)} %bitcast.8, ...), custom_call_target="tpu_custom_call" | custom-call | tf_op jit(solution)/shard_map/pallas_call | solution.py:514
  52.3 0.0 copy-start.1
  52.3 1.7 %copy.12 = bf16[128,1024]{1,0:T(8,128)(2,1)} copy(bf16[128,1024]{1,0:T(8,128)(2,1)} %get-tuple-element.8) | data formatting | bytes 524288
  53.9 0.0 copy-done.1
  53.9 0.5 copy.13
Async XLA Ops:
  0.6 0.7 %copy-start = (s32[64,2]{0,1:T(2,128)S(1)}, s32[64,2]{0,1:T(2,128)}, u32[]{:S(2)}) copy-start(s32[64,2]{0,1:T(2,128)} %param.11) | copy-start | bytes 1540
  52.3 1.7 %copy-start.1 = (f32[1,128]{1,0:T(1,128)S(1)}, f32[1,128]{1,0:T(1,128)}, u32[]{:S(2)}) copy-start(f32[1,128]{1,0:T(1,128)} %get-tuple-element.5) | copy-start | bytes 1540

commit v4 on v3

--- a/solution.py
+++ b/solution.py
@@ -405,9 +405,9 @@
         return carry
 
     lax.fori_loop(0, TOK - 1, step, 0)
+    encode(TOK - 1)
     for i in range(3, TOK):
         spread_grad(i)
-    encode(TOK - 1)
     back[t, j] = pieces[t, fc]
 
     own_delta[...] = jnp.zeros_like(own_delta)

time: 54.7 us -> 53.1 us (0.971)
  Pallas kernels: 50.2 us -> 48.5 us
    pallas_call x1, Pallas kernels: 50.2 us -> 48.5 us  [fused(): pl.pallas_call(functools.partial(kernel, pair, lat, tok), out_shape=(jax....]
where the time goes in v4:
time: 53.1 us; the launch traced here: 52.8 us
  Pallas kernels  48.5 us (91%)
  local copies, waits for them, and re-layouts  3.63 us (7%)
  between operations  0.66 us (1%)
    pallas_call x1, Pallas kernels, fused(): pl.pallas_call(functools.partial(kernel, pair, lat, tok), out_shape=(jax....  48.5 us
    unnamed x6, local copies, waits for them, and re-layouts  2.86 us

profile of v4, /device:TPU:0, one launch (start us, length us, event | category | flops | bytes accessed | tf_op | source)
XLA Modules:
  0.0 52.8 jit_solution(12932841136577191818)
XLA Ops:
  0.6 0.0 copy-start
  0.6 0.7 %copy-done = s32[64,2]{0,1:T(2,128)S(1)} copy-done((s32[64,2]{0,1:T(2,128)S(1)}, s32[64,2]{0,1:T(2,128)}, u32[]{:S(2)}) %copy-start) | copy-done | bytes 536
  1.3 0.1 broadcast_in_dim.9
  1.4 0.7 %reshape.7.act = s32[2,512]{1,0:T(2,128)} reshape(s32[2,64,8]{2,1,0:T(8,128)S(1)} %broadcast_in_dim.9) | data formatting | bytes 8192 | tf_op jit(solution)/shard_map/reshape | solution.py:509
  2.1 48.5 %shard_map.95 = (bf16[128,1024]{1,0:T(8,128)(2,1)}, f32[1,128]{1,0:T(1,128)}) custom-call(bf16[128,1024]{1,0:T(8,128)(2,1)} %bitcast.5, s32[1,128]{1,0:T(1,128)} %matches.1, bf16[128,1024]{1,0:T(8,128)(2,1)} %grad.1, s32[2,512]{1,0:T(2,128)} %reshape.7.act, bf16[4096,128]{1,0:T(8,128)(2,1)} %encoder.1, f32[1,128]{1,0:T(1,128)} %bitcast.8, ...), custom_call_target="tpu_custom_call" | custom-call | tf_op jit(solution)/shard_map/pallas_call | solution.py:514
  50.6 0.0 copy-start.1
  50.6 1.7 %copy.12 = bf16[128,1024]{1,0:T(8,128)(2,1)} copy(bf16[128,1024]{1,0:T(8,128)(2,1)} %get-tuple-element.8) | data formatting | bytes 524288
  52.3 0.0 copy-done.1
  52.3 0.5 copy.13
Async XLA Ops:
  0.6 0.7 %copy-start = (s32[64,2]{0,1:T(2,128)S(1)}, s32[64,2]{0,1:T(2,128)}, u32[]{:S(2)}) copy-start(s32[64,2]{0,1:T(2,128)} %param.11) | copy-start | bytes 1540
  50.6 1.7 %copy-start.1 = (f32[1,128]{1,0:T(1,128)S(1)}, f32[1,128]{1,0:T(1,128)}, u32[]{:S(2)}) copy-start(f32[1,128]{1,0:T(1,128)} %get-tuple-element.5) | copy-start | bytes 1540
